TPU v7x, 256 devices: a whole 4x4x8 slice. The times are simulated.
256 devices in a mesh: row: 8 (over y, x_lo), col: 32 (over z, x_hi, core).
Axes of the slice: x: 4 (x_hi: 2, x_lo: 2; x = x_hi * 2 + x_lo), y: 4, z: 8, core: 2. Of those that a mesh axis runs over, the one named last changes fastest.
Arguments:
- grad_out: bfloat16 [3072, 8192], P('row', 'col'), may hold values from -6 to 6
- gate_act: bfloat16 [3072, 28672], P('row', 'col'), may hold values from -6 to 6
- up_act: bfloat16 [3072, 28672], P('row', 'col'), may hold values from -6 to 6
- down_weight: bfloat16 [28672, 8192], P('col', 'row'), may hold values from -0.0625 to 0.0625
Outputs:
- grad_gate: bfloat16 [3072, 28672], P('row', 'col')
- grad_up: bfloat16 [3072, 28672], P('row', 'col')
- grad_weight: float32 [28672, 8192], P('col', 'row')
All inputs are finite; a program needn't handle non-finite values.
Results may differ from a plain program's by a relative error of at most 0.0028.
Values may be sent and summed in bfloat16 or wider, within the bound.
A program may use at most 128 MiB of HBM per device.

v0:
```python
import jax
import jax.numpy as jnp
from jax import lax
from jax.sharding import PartitionSpec as P


def collect_features(grad_out):
    return lax.all_gather(grad_out, "col", axis=1, tiled=True)


def on_device(grad_out, gate_act, up_act, down_weight):
    token_major = lax.all_to_all(
        collect_features(grad_out), "row", split_axis=1, concat_axis=0, tiled=True
    )
    grad_rows = collect_features(grad_out)
    grad_hidden = lax.dot_general(
        grad_rows,
        lax.all_gather(down_weight, "row", axis=1, tiled=True),
        (((1,), (1,)), ((), ())),
        preferred_element_type=jnp.float32,
    )
    gate_value = gate_act.astype(jnp.float32)
    up_value = up_act.astype(jnp.float32)
    sigmoid_gate = jax.nn.sigmoid(gate_value)
    swish = gate_value * sigmoid_gate
    grad_gate = (
        grad_hidden * up_value * sigmoid_gate * (1.0 + gate_value * (1.0 - sigmoid_gate))
    ).astype(jnp.bfloat16)
    grad_up = (grad_hidden * swish).astype(jnp.bfloat16)
    hidden = (swish * up_value).astype(jnp.bfloat16)
    grad_weight = lax.dot_general(
        lax.all_gather(hidden, "row", axis=0, tiled=True),
        token_major,
        (((0,), (0,)), ((), ())),
        preferred_element_type=jnp.float32,
    )
    return (grad_gate, grad_up, grad_weight)


def solution(mesh):
    placed = (P("row", "col"), P("row", "col"), P("row", "col"), P("col", "row"))
    return jax.shard_map(
        on_device,
        mesh=mesh,
        in_specs=placed,
        out_specs=(P("row", "col"), P("row", "col"), P("col", "row")),
        check_vma=False,
    )
```

profile of v0, /device:TPU:1, one launch (start us, length us, event | category | flops | bytes accessed | tf_op | source)
XLA Modules:
  0.0 607.0 jit_solution(11016101793268797252)
XLA Ops:
  7.2 0.0 all-gather.4.cloned.1.call-start
  7.2 1.7 copy.7
  9.0 0.0 all-gather.4.cloned.1.call-update
  9.0 0.0 all-gather.6.cloned.1.call-start
  9.0 0.7 all-gather.6.cloned.1.call-update
  9.7 0.0 all-gather.8.cloned.1.call-start
  9.8 99.5 %all-gather.4.cloned.1.call-done = bf16[384,8192]{0,1:T(8,128)(2,1)} async-done(((bf16[384,256]{0,1:T(8,128)(2,1)}), bf16[384,8192]{0,1:T(8,128)(2,1)}) %all-gather.4.cloned.1.call-update) | async-done | bytes 6291472 | tf_op jit(solution)/shard_map/all_gather | solution.py:8
  109.2 286.9 %all-gather.6.cloned.1.call-done = bf16[896,8192]{1,0:T(8,128)(2,1)} async-done(((bf16[896,1024]{1,0:T(8,128)(2,1)}), bf16[896,8192]{1,0:T(8,128)(2,1)}) %all-gather.6.cloned.1.call-update) | async-done | bytes 14680080 | tf_op jit(solution)/shard_map/all_gather | solution.py:18
  396.1 13.8 %multiply_convert_fusion = (bf16[384,896]{1,0:T(8,128)(2,1)}, bf16[384,896]{1,0:T(8,128)(2,1)}, bf16[384,896]{1,0:T(8,128)(2,1)}) fusion(bf16[384,896]{1,0:T(8,128)(2,1)} %param.5, bf16[384,896]{1,0:T(8,128)(2,1)} %param.6, bf16[384,8192]{0,1:T(8,128)(2,1)} %all-gather.4.cloned.1.call-done, bf16[896,8192]{1,0:T(8,128)(2,1)} %all-gather.6.cloned.1.call-done), kind=kOutput, calls=%fused_computation.13 | convolution fusion | flops 5642993664 | bytes 24412160 | tf_op jit(solution)/shard_map/dot_general | solution.py:16
  409.9 0.0 all-gather.8.cloned.1.call-update
  409.9 136.3 %all_to_all.19 = bf16[384,8,1024]{0,2,1:T(8,128)(2,1)} all-to-all(bf16[384,8,1024]{0,2,1:T(8,128)(2,1)} %bitcast.8), channel_id=1, replica_groups=mesh['row'=8,'col'=32] {'row'}, dimensions={1} | all-to-all | bytes 12582912 | tf_op jit(solution)/shard_map/all_to_all | solution.py:12
  546.2 8.6 %copy.8 = bf16[8,384,1024]{2,1,0:T(8,128)(2,1)} copy(bf16[8,384,1024]{1,2,0:T(8,128)(2,1)} %bitcast.7) | data formatting | bytes 12582912 | tf_op jit(solution)/shard_map/all_to_all | solution.py:12
  554.9 34.7 %all-gather.8.cloned.1.call-done = bf16[3072,896]{1,0:T(8,128)(2,1)} async-done(((bf16[384,896]{1,0:T(8,128)(2,1)}), bf16[3072,896]{1,0:T(8,128)(2,1)}) %all-gather.8.cloned.1.call-update) | async-done | bytes 5505040 | tf_op jit(solution)/shard_map/all_gather | solution.py:32
  589.6 10.8 %fusion.8 = f32[896,1024]{1,0:T(8,128)} fusion(bf16[3072,896]{1,0:T(8,128)(2,1)} %all-gather.8.cloned.1.call-done, bf16[3072,1024]{1,0:T(8,128)(2,1)} %bitcast.9), kind=kOutput, calls=%fused_computation.14 | convolution fusion | flops 5637144576 | bytes 15466496 | tf_op jit(solution)/shard_map/dot_general | solution.py:31
Async XLA Ops:
  7.2 102.1 %all-gather.4.cloned.1.call-start = ((), (), s32[]{:S(2)}) async-start(), calls=%async_computation.1 | async-start | bytes 6488064 | tf_op jit(solution)/shard_map/all_gather | solution.py:8
  9.0 387.1 %all-gather.6.cloned.1.call-start = ((), (), s32[]{:S(2)}) async-start(), calls=%async_computation.2 | async-start | bytes 16515072 | tf_op jit(solution)/shard_map/all_gather | solution.py:18
  9.7 579.9 %all-gather.8.cloned.1.call-start = ((), (), s32[]{:S(2)}) async-start(), calls=%async_computation.3 | async-start | bytes 6193152 | tf_op jit(solution)/shard_map/all_gather | solution.py:32
Sparse Core Ops, SparseCore 0:
  11.3 97.8 all-gather.3
  111.0 285.0 all-gather.5
  410.1 179.5 all-gather.7
where the time goes:
time: 607 us
  waiting for transfers between devices  422 us (70%)
  blocking collectives  136 us (22%)
  matrix products  24.7 us (4%)
  between operations  13.7 us (2%)
  local copies, waits for them, and re-layouts  10.4 us (2%)
    all_gather x1, waiting for transfers between devices, on_device(): lax.all_gather(down_weight, 'row', axis=1, tiled=True)  287 us
    all_to_all x1, blocking collectives, on_device(): lax.all_to_all(collect_features(grad_out), 'row', split_axis=1, concat_ax...  136 us
    all_gather x1, waiting for transfers between devices, collect_features(): return lax.all_gather(grad_out, 'col', axis=1, tiled=True)  99.5 us
    all_gather x1, waiting for transfers between devices, on_device(): lax.all_gather(hidden, 'row', axis=0, tiled=True)  34.7 us
    dot_general x1, matrix products, on_device(): lax.dot_general(grad_rows, lax.all_gather(down_weight, 'row', axis=1, til...  13.8 us
  transfers between devices with their start and end apart: 3, of which 3 were waited for; matrix products, arithmetic and copies ran while one was open for 1% of the time, Pallas kernels for 0%

commit v1 on v0

--- a/solution.py
+++ b/solution.py
@@ -4,8 +4,15 @@
 from jax.sharding import PartitionSpec as P
 
 
+def _perform_stacks_all(block_here):
+    response = jnp.concatenate(
+        lax.all_to_all(jnp.stack(lax.psum(1, "col") * [block_here], axis=0), "col", 0, 0), axis=1
+    )
+    return response
+
+
 def collect_features(grad_out):
-    return lax.all_gather(grad_out, "col", axis=1, tiled=True)
+    return _perform_stacks_all(grad_out)
 
 
 def on_device(grad_out, gate_act, up_act, down_weight):

time: 607 us -> 579 us (0.954)
  waiting for transfers between devices: 422 us -> 240 us
  blocking collectives: 136 us -> 290 us
    all_to_all x0 -> x1, blocking collectives: none -> 153 us  [_perform_stacks_all(): lax.all_to_all(jnp.stack(lax.psum(1, 'col') * [block_here], axis=0), 'col...]
    all_gather x1 -> x0, waiting for transfers between devices: 99.5 us -> none  [collect_features(): return lax.all_gather(grad_out, 'col', axis=1, tiled=True)]
    all_gather x1, waiting for transfers between devices: 287 us -> 204 us  [on_device(): lax.all_gather(down_weight, 'row', axis=1, tiled=True)]
  transfers between devices with their start and end apart: 3 -> 2, of which waited for: 3 -> 2; matrix products, arithmetic and copies ran while one was open for 1% -> 2% of each run, Pallas kernels for 0% -> 0%
where the time goes in v1:
time: 579 us
  blocking collectives  290 us (50%)
  waiting for transfers between devices  240 us (41%)
  matrix products  24.5 us (4%)
  between operations  14.1 us (2%)
  local copies, waits for them, and re-layouts  10.7 us (2%)
    all_gather x1, waiting for transfers between devices, on_device(): lax.all_gather(down_weight, 'row', axis=1, tiled=True)  204 us
    all_to_all x1, blocking collectives, _perform_stacks_all(): lax.all_to_all(jnp.stack(lax.psum(1, 'col') * [block_here], axis=0), 'col...  153 us
    all_to_all x1, blocking collectives, on_device(): lax.all_to_all(collect_features(grad_out), 'row', split_axis=1, concat_ax...  137 us
    all_gather x1, waiting for transfers between devices, on_device(): lax.all_gather(hidden, 'row', axis=0, tiled=True)  34.9 us
    dot_general x1, matrix products, on_device(): lax.dot_general(grad_rows, lax.all_gather(down_weight, 'row', axis=1, til...  13.6 us
  transfers between devices with their start and end apart: 2, of which 2 were waited for; matrix products, arithmetic and copies ran while one was open for 2% of the time, Pallas kernels for 0%

profile of v1, /device:TPU:1, one launch (start us, length us, event | category | flops | bytes accessed | tf_op | source)
XLA Modules:
  0.0 578.8 jit_solution(2369960090843476481)
XLA Ops:
  7.2 0.0 all-gather.3.cloned.1.call-start
  7.2 0.7 all-gather.3.cloned.1.call-update
  7.9 0.0 all-gather.5.cloned.1.call-start
  7.9 1.1 copy.7
  9.0 0.9 stack.2
  10.0 0.0 copy-start
  10.0 0.0 copy-start.1
  10.0 153.0 %all_to_all.25 = bf16[32,384,256]{1,2,0:T(8,128)(2,1)} all-to-all(bf16[32,384,256]{1,2,0:T(8,128)(2,1)S(1)} %stack.2), channel_id=1, replica_groups=mesh['row'=8,'col'=32] {'col'}, dimensions={0} | all-to-all | bytes 12582912 | tf_op jit(solution)/shard_map/all_to_all | solution.py:9
  163.0 204.3 %all-gather.3.cloned.1.call-done = bf16[896,8192]{1,0:T(8,128)(2,1)} async-done(((bf16[896,1024]{1,0:T(8,128)(2,1)}), bf16[896,8192]{1,0:T(8,128)(2,1)}) %all-gather.3.cloned.1.call-update) | async-done | bytes 14680080 | tf_op jit(solution)/shard_map/all_gather | solution.py:25
  367.3 0.0 copy-done
  367.3 0.0 copy-done.1
  367.3 13.6 %multiply_convert_fusion = (bf16[384,896]{1,0:T(8,128)(2,1)}, bf16[384,896]{1,0:T(8,128)(2,1)}, bf16[384,896]{1,0:T(8,128)(2,1)}) fusion(bf16[384,896]{1,0:T(8,128)(2,1)S(1)} %copy-done, bf16[384,896]{1,0:T(8,128)(2,1)S(1)} %copy-done.1, bf16[384,8192]{0,1:T(8,128)(2,1)} %bitcast.11, bf16[896,8192]{1,0:T(8,128)(2,1)} %all-gather.3.cloned.1.call-done), kind=kOutput, calls=%fused_computation.13 | convolution fusion | flops 5642993664 | bytes 24412160 | tf_op jit(solution)/shard_map/dot_general | solution.py:23
  380.9 0.0 all-gather.5.cloned.1.call-update
  381.0 136.7 %all_to_all.26 = bf16[384,8,1024]{0,2,1:T(8,128)(2,1)} all-to-all(bf16[384,8,1024]{0,2,1:T(8,128)(2,1)} %bitcast.12), channel_id=1, replica_groups=mesh['row'=8,'col'=32] {'row'}, dimensions={1} | all-to-all | bytes 12582912 | tf_op jit(solution)/shard_map/all_to_all | solution.py:19
  517.6 8.6 %copy.8 = bf16[8,384,1024]{2,1,0:T(8,128)(2,1)} copy(bf16[8,384,1024]{1,2,0:T(8,128)(2,1)} %bitcast.13) | data formatting | bytes 12582912 | tf_op jit(solution)/shard_map/all_to_all | solution.py:19
  526.2 34.9 %all-gather.5.cloned.1.call-done = bf16[3072,896]{1,0:T(8,128)(2,1)} async-done(((bf16[384,896]{1,0:T(8,128)(2,1)}), bf16[3072,896]{1,0:T(8,128)(2,1)}) %all-gather.5.cloned.1.call-update) | async-done | bytes 5505040 | tf_op jit(solution)/shard_map/all_gather | solution.py:39
  561.1 10.8 %fusion.8 = f32[896,1024]{1,0:T(8,128)} fusion(bf16[3072,896]{1,0:T(8,128)(2,1)} %all-gather.5.cloned.1.call-done, bf16[3072,1024]{1,0:T(8,128)(2,1)} %bitcast.14), kind=kOutput, calls=%fused_computation.14 | convolution fusion | flops 5637144576 | bytes 15466496 | tf_op jit(solution)/shard_map/dot_general | solution.py:38
Async XLA Ops:
  7.2 360.1 %all-gather.3.cloned.1.call-start = ((), (), s32[]{:S(2)}) async-start(), calls=%async_computation.2 | async-start | bytes 16515072 | tf_op jit(solution)/shard_map/all_gather | solution.py:25
  7.9 553.2 %all-gather.5.cloned.1.call-start = ((), (), s32[]{:S(2)}) async-start(), calls=%async_computation.3 | async-start | bytes 6193152 | tf_op jit(solution)/shard_map/all_gather | solution.py:39
  10.0 357.3 %copy-start = (bf16[384,896]{1,0:T(8,128)(2,1)S(1)}, bf16[384,896]{1,0:T(8,128)(2,1)}, u32[]{:S(2)}) copy-start(bf16[384,896]{1,0:T(8,128)(2,1)} %param.5) | copy-start | bytes 2064388
  10.0 357.3 %copy-start.1 = (bf16[384,896]{1,0:T(8,128)(2,1)S(1)}, bf16[384,896]{1,0:T(8,128)(2,1)}, u32[]{:S(2)}) copy-start(bf16[384,896]{1,0:T(8,128)(2,1)} %param.6) | copy-start | bytes 2064388
Sparse Core Ops, SparseCore 0:
  9.8 357.4 all-gather.2
  381.1 179.9 all-gather.4
